TPU v7x, 32 devices: a whole 2x2x4 slice. The times are simulated.
32 devices in a mesh: gx: 2 (over x), gy: 4 (over z), gz: 4 (over y, core).
Axes of the slice: x: 2, y: 2, z: 4, core: 2. Of those that a mesh axis runs over, the one named last changes fastest.
Arguments:
- volume: float32 [16, 8, 64, 512], P(None, 'gx', 'gy', 'gz'), may hold values from -26 to 26
- weight: float32 [16, 16, 3, 3, 3], replicated, may hold values from -0.3125 to 0.3125
- gamma: float32 [16], replicated, may hold values from 0.5 to 1.5
- beta: float32 [16], replicated, may hold values from -0.5 to 0.5
- cotangent: float32 [16, 8, 64, 512], P(None, 'gx', 'gy', 'gz'), may hold values from -6 to 6
Outputs:
- input_grad: float32 [16, 8, 64, 512], P(None, 'gx', 'gy', 'gz')
- weight_grad: float32 [16, 16, 3, 3, 3], replicated
- gamma_grad: float32 [16], replicated
- beta_grad: float32 [16], replicated
All inputs are finite; a program needn't handle non-finite values.
Results may differ from a plain program's by a relative error of at most 0.0003.
Values sent between devices are 32-bit elements; how exact they have to be, the bound alone decides.
No kernel may reach another device: no remote copies, remote signals or barrier semaphores. Data moves between devices by JAX's collectives and lax.ppermute only.
A program may use at most 64 MiB of HBM per device.

v0:
```python
import jax
import jax.numpy as jnp
from jax import lax
from jax.sharding import PartitionSpec as P


def with_halo(block, sides, width):
    for axis, dim in sides:
        count = lax.axis_size(axis)
        forward = [(i, i + 1) for i in range(count - 1)]
        forward.append((count - 1, 0))
        backward = [(target, source) for source, target in forward]
        low = lax.ppermute(
            lax.slice_in_dim(block, block.shape[dim] - width, None, axis=dim), axis, forward
        )
        high = lax.ppermute(lax.slice_in_dim(block, 0, width, axis=dim), axis, backward)
        block = jnp.concatenate([low, block, high], axis=dim)
    return block


def mix(kernel, slab):
    return jnp.einsum("oi,ixyz->oxyz", kernel, slab, precision=lax.Precision.HIGHEST)


def contract(left, slab):
    return jnp.einsum("oxyz,ixyz->oi", left, slab, precision=lax.Precision.HIGHEST)


def shards(volume, weight, gamma, beta, cotangent):
    chans, cells_x, cells_y, cells_z = volume.shape
    count = float(
        cells_x
        * cells_y
        * cells_z
        * lax.axis_size("gx")
        * lax.axis_size("gy")
        * lax.axis_size("gz")
    )
    padded = with_halo(volume, (("gx", 1), ("gy", 2), ("gz", 3)), 1)

    def window(source, first, second, third):
        return source[
            :, first : first + cells_x, second : second + cells_y, third : third + cells_z
        ]

    conv = jnp.zeros(volume.shape, jnp.float32)
    for first in range(3):
        for second in range(3):
            for third in range(3):
                conv = conv + mix(
                    weight[:, :, first, second, third], window(padded, first, second, third)
                )
    first_sum, square_sum = lax.psum(
        (jnp.sum(conv, axis=(1, 2, 3)), jnp.sum(conv * conv, axis=(1, 2, 3))), ("gx", "gy", "gz")
    )
    mean = first_sum / count
    var = square_sum / count - mean * mean
    centred = conv - mean[:, None, None, None]
    rstd = lax.rsqrt(var + 1e-05)
    normed = centred * rstd[:, None, None, None]
    act = gamma[:, None, None, None] * normed + beta[:, None, None, None]
    sig = jax.nn.sigmoid(act)
    act_grad = cotangent * sig * (1.0 + act * (1.0 - sig))
    scale = gamma * rstd
    gamma_grad, beta_grad = lax.psum(
        (jnp.sum(act_grad * normed, axis=(1, 2, 3)), jnp.sum(act_grad, axis=(1, 2, 3))),
        ("gx", "gy", "gz"),
    )
    conv_grad = scale[:, None, None, None] * (
        act_grad
        - (beta_grad / count)[:, None, None, None]
        - normed * (gamma_grad / count)[:, None, None, None]
    )
    pieces = []
    for first in range(3):
        for second in range(3):
            for third in range(3):
                pieces.append(contract(conv_grad, window(padded, first, second, third)))
    weight_grad = lax.psum(
        jnp.stack(pieces, axis=2).reshape(chans, chans, 3, 3, 3), ("gx", "gy", "gz")
    )
    grad_padded = with_halo(conv_grad, (("gx", 1), ("gy", 2), ("gz", 3)), 1)
    input_grad = jnp.zeros(volume.shape, jnp.float32)
    for first in range(3):
        for second in range(3):
            for third in range(3):
                input_grad = input_grad + mix(
                    weight[:, :, first, second, third].T,
                    window(grad_padded, 2 - first, 2 - second, 2 - third),
                )
    return (input_grad, weight_grad, gamma_grad, beta_grad)


def solution(mesh):
    return jax.shard_map(
        shards,
        mesh=mesh,
        in_specs=(P(None, "gx", "gy", "gz"), P(), P(), P(), P(None, "gx", "gy", "gz")),
        out_specs=(P(None, "gx", "gy", "gz"), P(), P(), P()),
        check_vma=False,
    )
```

profile of v0, /device:TPU:0, one launch (start us, length us, event | category | flops | bytes accessed | tf_op | source)
XLA Modules:
  0.0 250.0 jit_solution(15097560473422288166)
XLA Ops:
  0.6 1.1 fusion.319
  1.7 3.0 %collective-permute-start = (f32[16,1,16,128]{3,0,2,1:T(8,128)S(1)}, f32[16,1,16,128]{3,0,2,1:T(8,128)S(1)}, u32[]{:S(2)}, u32[]{:S(2)}) collective-permute-start(f32[16,1,16,128]{3,0,2,1:T(8,128)S(1)} %copy.207), channel_id=1, source_target_pairs={{0,16},{16,0},{1,17},{17,1},{2,18},{18,2},{3,19},{19,3},{4,20},{20... | collective-permute-start | bytes 393224 | tf_op jit(solution)/shard_map/ppermute | solution.py:13
  4.9 2.7 %fusion.206 = f32[16,4,16,128]{3,0,2,1:T(8,128)} fusion(f32[16,16,3,3,3]{1,0,4,3,2:T(8,128)} %param.6, f32[16,4,16,128]{3,2,1,0:T(8,128)} %param.5), kind=kOutput, calls=%fused_computation.290 | convolution fusion | flops 25165824 | bytes 1056768 | tf_op jit(solution)/shard_map/oi,ixyz->oxyz/dot_general | solution.py:22
  7.6 1.5 collective-permute-done
  9.5 1.6 collective-permute-done.1
  11.1 1.9 collective-permute-start.2
  13.0 2.1 collective-permute-start.3
  15.1 2.1 fusion.225
  17.2 2.1 convolution_bitcast_fusion.4
  21.0 1.9 collective-permute-start.5
  22.9 2.1 fusion.85
  25.0 2.1 fusion.86
  27.1 2.1 fusion.87
  29.1 2.1 convolution_bitcast_fusion.3
  31.2 2.1 convolution_bitcast_fusion.5
  33.3 2.1 convolution_bitcast_fusion.6
  36.1 1.6 copy.51
  37.7 1.8 maximum_maximum_fusion
  47.1 1.1 convolution_bitcast_fusion.18
  50.1 1.0 fusion.44
  51.6 1.2 fusion.312
  52.8 38.9 %all-reduce.1 = (f32[16]{0:T(128)S(1)}, f32[16]{0:T(128)S(1)}) all-reduce(f32[16]{0:T(128)S(1)} %get-tuple-element.15, f32[16]{0:T(128)S(1)} %get-tuple-element.14), channel_id=1, replica_groups=mesh['gx'=2,'gy'=4,'gz'=4] {'gx','gy','gz'}, use_global_device_ids=true, to_apply=%region_1.0 | all-reduce | flops 32 | bytes 256 | tf_op jit(solution)/shard_map/psum | solution.py:53
  91.7 2.4 fusion.311
  94.1 40.5 %all-reduce = (f32[16]{0:T(128)S(1)}, f32[16]{0:T(128)S(1)}) all-reduce(f32[16]{0:T(128)S(1)} %get-tuple-element.13, f32[16]{0:T(128)S(1)} %get-tuple-element.12), channel_id=1, replica_groups=mesh['gx'=2,'gy'=4,'gz'=4] {'gx','gy','gz'}, use_global_device_ids=true, to_apply=%region_7.0 | all-reduce | flops 32 | bytes 256 | tf_op jit(solution)/shard_map/psum | solution.py:65
  134.6 1.4 subtract_multiply_fusion
  147.4 1.0 fusion.64
  160.2 41.9 %psum.39 = f32[16,16,3,3,3]{1,0,4,3,2:T(8,128)} all-reduce(f32[16,16,3,3,3]{1,0,4,3,2:T(8,128)} %bitcast.644), channel_id=1, replica_groups=mesh['gx'=2,'gy'=4,'gz'=4] {'gx','gy','gz'}, use_global_device_ids=true, to_apply=%region_8.0 | all-reduce | flops 6912 | bytes 55296 | tf_op jit(solution)/shard_map/psum | solution.py:79
  202.1 1.6 collective-permute-start.6
  204.2 1.4 fusion.204
  205.6 2.5 collective-permute-done.6
  208.0 1.4 collective-permute-done.7
  209.4 2.2 collective-permute-start.9
  211.7 1.4 fusion.78
  213.7 3.9 %collective-permute-done.8 = f32[16,6,1,128]{3,0,2,1:T(8,128)S(1)} collective-permute-done((f32[16,6,1,128]{3,0,2,1:T(8,128)S(1)}, f32[16,6,1,128]{3,0,2,1:T(8,128)S(1)}, u32[]{:S(2)}, u32[]{:S(2)}) %collective-permute-start.8) | collective-permute-done | bytes 49184 | tf_op jit(solution)/shard_map/ppermute | solution.py:13
  217.6 1.2 fusion.315
  218.8 1.8 copy.56
  221.9 1.4 fusion.177
  223.3 1.4 fusion.175
  224.7 1.4 fusion.176
  226.1 1.4 fusion.174
  227.5 1.4 convolution_bitcast_fusion.2
  228.9 1.4 convolution_bitcast_fusion
  230.3 1.6 copy.57
  231.9 1.6 copy.61
  233.5 2.0 pad_maximum_fusion.3
  246.5 1.1 fusion.46
  247.8 1.0 fusion.48
  248.8 1.0 copy.88
  (158 shorter events, 49.1 us)
Async XLA Ops:
  0.6 8.5 %copy-start.2 = (f32[16,4,16,128]{3,2,1,0:T(8,128)S(1)}, f32[16,4,16,128]{3,2,1,0:T(8,128)}, u32[]{:S(2)}) copy-start(f32[16,4,16,128]{3,2,1,0:T(8,128)} %param.5) | copy-start | bytes 1572868
  1.7 7.4 %collective-permute-start = (f32[16,1,16,128]{3,0,2,1:T(8,128)S(1)}, f32[16,1,16,128]{3,0,2,1:T(8,128)S(1)}, u32[]{:S(2)}, u32[]{:S(2)}) collective-permute-start(f32[16,1,16,128]{3,0,2,1:T(8,128)S(1)} %copy.207), channel_id=1, source_target_pairs={{0,16},{16,0},{1,17},{17,1},{2,18},{18,2},{3,19},{19,3},{4,20},{20... | collective-permute-start | bytes 393224 | tf_op jit(solution)/shard_map/ppermute | solution.py:13
  4.8 6.3 %collective-permute-start.1 = (f32[16,1,16,128]{3,0,2,1:T(8,128)S(1)}, f32[16,1,16,128]{3,0,2,1:T(8,128)S(1)}, u32[]{:S(2)}, u32[]{:S(2)}) collective-permute-start(f32[16,1,16,128]{3,0,2,1:T(8,128)S(1)} %copy.208), channel_id=1, source_target_pairs={{16,0},{0,16},{17,1},{1,17},{18,2},{2,18},{19,3},{3,19},{20,4},{4,... | collective-permute-start | bytes 393224 | tf_op jit(solution)/shard_map/ppermute | solution.py:16
  9.5 9.7 %copy-start.7 = (f32[16,5,16,128]{3,0,2,1:T(8,128)}, f32[16,5,16,128]{3,0,2,1:T(8,128)S(1)}, u32[]{:S(2)}) copy-start(f32[16,5,16,128]{3,0,2,1:T(8,128)S(1)} %get-tuple-element.37) | copy-start | bytes 1966084
  11.1 8.1 %copy-start.5 = (f32[16,5,16,128]{3,0,2,1:T(8,128)}, f32[16,5,16,128]{3,0,2,1:T(8,128)S(1)}, u32[]{:S(2)}) copy-start(f32[16,5,16,128]{3,0,2,1:T(8,128)S(1)} %get-tuple-element.44) | copy-start | bytes 1966084
  11.1 8.1 %collective-permute-start.2 = (f32[16,6,1,128]{3,0,2,1:T(8,128)S(1)}, f32[16,6,1,128]{3,0,2,1:T(8,128)S(1)}, u32[]{:S(2)}, u32[]{:S(2)}) collective-permute-start(f32[16,6,1,128]{3,0,2,1:T(8,128)S(1)} %get-tuple-element.33), channel_id=1, source_target_pairs={{0,4},{4,8},{8,12},{12,0},{1,5},{5,9},{9,13},{13,1},{2,6},{6,10},{... | collective-permute-start | bytes 147464 | tf_op jit(solution)/shard_map/ppermute | solution.py:13
  13.0 6.2 %collective-permute-start.3 = (f32[16,6,1,128]{3,0,2,1:T(8,128)S(1)}, f32[16,6,1,128]{3,0,2,1:T(8,128)S(1)}, u32[]{:S(2)}, u32[]{:S(2)}) collective-permute-start(f32[16,6,1,128]{3,0,2,1:T(8,128)S(1)} %get-tuple-element.34), channel_id=1, source_target_pairs={{4,0},{8,4},{12,8},{0,12},{5,1},{9,5},{13,9},{1,13},{6,2},{10,6},{... | collective-permute-start | bytes 147464 | tf_op jit(solution)/shard_map/ppermute | solution.py:16
  20.3 15.1 %collective-permute-start.4 = (f32[16,6,18,1]{2,0,3,1:T(8,128)S(1)}, f32[16,6,18,1]{2,0,3,1:T(8,128)S(1)}, u32[]{:S(2)}, u32[]{:S(2)}) collective-permute-start(f32[16,6,18,1]{2,0,3,1:T(8,128)S(1)} %copy.48), channel_id=1, source_target_pairs={{0,1},{1,2},{2,3},{3,0},{4,5},{5,6},{6,7},{7,4},{8,9},{9,10},{10,1... | collective-permute-start | bytes 20744 | tf_op jit(solution)/shard_map/ppermute | solution.py:13
  21.0 15.1 %collective-permute-start.5 = (f32[16,6,18,1]{2,0,3,1:T(8,128)S(1)}, f32[16,6,18,1]{2,0,3,1:T(8,128)S(1)}, u32[]{:S(2)}, u32[]{:S(2)}) collective-permute-start(f32[16,6,18,1]{2,0,3,1:T(8,128)S(1)} %copy.50), channel_id=1, source_target_pairs={{1,0},{2,1},{3,2},{0,3},{5,4},{6,5},{7,6},{4,7},{9,8},{10,9},{11,1... | collective-permute-start | bytes 20744 | tf_op jit(solution)/shard_map/ppermute | solution.py:16
  37.7 1.8 copy-start.26
  39.5 11.6 %copy-start = (f32[16,6,18,129]{3,0,2,1:T(8,128)}, f32[16,6,18,129]{3,0,2,1:T(8,128)S(1)}, u32[]{:S(2)}) copy-start(f32[16,6,18,129]{3,0,2,1:T(8,128)S(1)} %get-tuple-element.28) | copy-start | bytes 2674948
  48.2 1.9 copy-start.11
  48.2 1.9 copy-start.12
  48.2 1.9 copy-start.23
  48.2 1.9 copy-start.24
  48.2 1.9 copy-start.25
  50.1 1.0 copy-start.9
  50.1 1.2 copy-start.17
  50.1 1.3 copy-start.18
  50.1 1.5 copy-start.19
  51.6 40.1 %copy-start.31 = (f32[16]{0:T(128)S(1)}, f32[16]{0:T(128)}, u32[]{:S(2)}) copy-start(f32[16]{0:T(128)} %param.7) | copy-start | bytes 196
  51.6 40.1 %copy-start.32 = (f32[16]{0:T(128)S(1)}, f32[16]{0:T(128)}, u32[]{:S(2)}) copy-start(f32[16]{0:T(128)} %param.8) | copy-start | bytes 196
  52.8 81.8 %copy-start.4 = (f32[16,4,16,128]{3,0,2,1:T(8,128)}, f32[16,4,16,128]{3,0,2,1:T(8,128)S(1)}, u32[]{:S(2)}) copy-start(f32[16,4,16,128]{3,0,2,1:T(8,128)S(1)} %get-tuple-element.47) | copy-start | bytes 1572868
  134.6 3.7 %copy-start.33 = (f32[16]{0:T(128)}, f32[16]{0:T(128)S(1)}, u32[]{:S(2)}) copy-start(f32[16]{0:T(128)S(1)} %get-tuple-element.16) | copy-start | bytes 196
  134.6 3.7 %copy-start.34 = (f32[16]{0:T(128)}, f32[16]{0:T(128)S(1)}, u32[]{:S(2)}) copy-start(f32[16]{0:T(128)S(1)} %get-tuple-element.17) | copy-start | bytes 196
  136.0 2.3 copy-start.1
  137.5 2.5 %copy-start.8 = (f32[16,5,16,128]{3,0,2,1:T(8,128)S(1)}, f32[16,5,16,128]{3,0,2,1:T(8,128)}, u32[]{:S(2)}) copy-start(f32[16,5,16,128]{3,0,2,1:T(8,128)} %copy-done.7) | copy-start | bytes 1966084
  145.0 2.5 copy-start.3
  152.6 2.5 %copy-start.6 = (f32[16,5,16,128]{3,0,2,1:T(8,128)S(1)}, f32[16,5,16,128]{3,0,2,1:T(8,128)}, u32[]{:S(2)}) copy-start(f32[16,5,16,128]{3,0,2,1:T(8,128)} %copy-done.5) | copy-start | bytes 1966084
  157.0 47.2 %copy-start.27 = (f32[16,16,3,3,3]{1,0,4,3,2:T(8,128)S(1)}, f32[16,16,3,3,3]{1,0,4,3,2:T(8,128)}, u32[]{:S(2)}) copy-start(f32[16,16,3,3,3]{1,0,4,3,2:T(8,128)} %param.6) | copy-start | bytes 82948
  157.8 44.3 %copy-start.30 = (f32[16,1,16,128]{3,0,2,1:T(8,128)S(1)}, f32[16,1,16,128]{3,0,2,1:T(8,128)}, u32[]{:S(2)}) copy-start(f32[16,1,16,128]{3,0,2,1:T(8,128)} %get-tuple-element.35) | copy-start | bytes 393220
  157.8 45.9 %copy-start.29 = (f32[16,1,16,128]{3,0,2,1:T(8,128)S(1)}, f32[16,1,16,128]{3,0,2,1:T(8,128)}, u32[]{:S(2)}) copy-start(f32[16,1,16,128]{3,0,2,1:T(8,128)} %get-tuple-element.36) | copy-start | bytes 393220
  159.5 0.7 copy-start.28
  202.1 5.9 %collective-permute-start.6 = (f32[16,1,16,128]{3,0,2,1:T(8,128)S(1)}, f32[16,1,16,128]{3,0,2,1:T(8,128)S(1)}, u32[]{:S(2)}, u32[]{:S(2)}) collective-permute-start(f32[16,1,16,128]{3,0,2,1:T(8,128)S(1)} %copy-done.30), channel_id=1, source_target_pairs={{0,16},{16,0},{1,17},{17,1},{2,18},{18,2},{3,19},{19,3},{4,20},{20... | collective-permute-start | bytes 393224 | tf_op jit(solution)/shard_map/ppermute | solution.py:13
  203.7 5.7 %collective-permute-start.7 = (f32[16,1,16,128]{3,0,2,1:T(8,128)S(1)}, f32[16,1,16,128]{3,0,2,1:T(8,128)S(1)}, u32[]{:S(2)}, u32[]{:S(2)}) collective-permute-start(f32[16,1,16,128]{3,0,2,1:T(8,128)S(1)} %copy-done.29), channel_id=1, source_target_pairs={{16,0},{0,16},{17,1},{1,17},{18,2},{2,18},{19,3},{3,19},{20,4},{4,... | collective-permute-start | bytes 393224 | tf_op jit(solution)/shard_map/ppermute | solution.py:16
  209.4 4.2 %collective-permute-start.9 = (f32[16,6,1,128]{3,0,2,1:T(8,128)S(1)}, f32[16,6,1,128]{3,0,2,1:T(8,128)S(1)}, u32[]{:S(2)}, u32[]{:S(2)}) collective-permute-start(f32[16,6,1,128]{3,0,2,1:T(8,128)S(1)} %get-tuple-element.32), channel_id=1, source_target_pairs={{4,0},{8,4},{12,8},{0,12},{5,1},{9,5},{13,9},{1,13},{6,2},{10,6},{... | collective-permute-start | bytes 147464 | tf_op jit(solution)/shard_map/ppermute | solution.py:16
  211.7 5.9 %collective-permute-start.8 = (f32[16,6,1,128]{3,0,2,1:T(8,128)S(1)}, f32[16,6,1,128]{3,0,2,1:T(8,128)S(1)}, u32[]{:S(2)}, u32[]{:S(2)}) collective-permute-start(f32[16,6,1,128]{3,0,2,1:T(8,128)S(1)} %get-tuple-element.31), channel_id=1, source_target_pairs={{0,4},{4,8},{8,12},{12,0},{1,5},{5,9},{9,13},{13,1},{2,6},{6,10},{... | collective-permute-start | bytes 147464 | tf_op jit(solution)/shard_map/ppermute | solution.py:13
  220.7 9.7 %collective-permute-start.10 = (f32[16,6,18,1]{2,0,3,1:T(8,128)S(1)}, f32[16,6,18,1]{2,0,3,1:T(8,128)S(1)}, u32[]{:S(2)}, u32[]{:S(2)}) collective-permute-start(f32[16,6,18,1]{2,0,3,1:T(8,128)S(1)} %copy.56), channel_id=1, source_target_pairs={{1,0},{2,1},{3,2},{0,3},{5,4},{6,5},{7,6},{4,7},{9,8},{10,9},{11,1... | collective-permute-start | bytes 20744 | tf_op jit(solution)/shard_map/ppermute | solution.py:16
  221.4 10.6 %collective-permute-start.11 = (f32[16,6,18,1]{2,0,3,1:T(8,128)S(1)}, f32[16,6,18,1]{2,0,3,1:T(8,128)S(1)}, u32[]{:S(2)}, u32[]{:S(2)}) collective-permute-start(f32[16,6,18,1]{2,0,3,1:T(8,128)S(1)} %copy.60), channel_id=1, source_target_pairs={{0,1},{1,2},{2,3},{3,0},{4,5},{5,6},{6,7},{7,4},{8,9},{9,10},{10,1... | collective-permute-start | bytes 20744 | tf_op jit(solution)/shard_map/ppermute | solution.py:13
  244.1 2.3 copy-start.10
  244.1 2.3 copy-start.13
  244.1 2.3 copy-start.20
  244.3 2.1 copy-start.21
  244.3 2.1 copy-start.22
  246.4 1.1 copy-start.14
  246.4 1.2 copy-start.15
  246.4 1.3 copy-start.16
where the time goes:
time: 255 us; the launch traced here: 250 us
  blocking collectives  121 us (47%)
  matrix products  78.7 us (31%)
  local copies, waits for them, and re-layouts  15.7 us (6%)
  starting transfers between devices  13.8 us (5%)
  waiting for transfers between devices  10.9 us (4%)
  other arithmetic  7.77 us (3%)
    dot_general x54, matrix products, mix(): jnp.einsum('oi,ixyz->oxyz', kernel, slab, precision=lax.Precision.HIGHEST)  56 us
    psum x1, blocking collectives, shards(): lax.psum(jnp.stack(pieces, axis=2).reshape(chans, chans, 3, 3, 3), ('gx',...  41.9 us
    psum x1, blocking collectives, shards(): lax.psum((jnp.sum(act_grad * normed, axis=(1, 2, 3)), jnp.sum(act_grad, a...  40.5 us
    psum x1, blocking collectives, shards(): lax.psum((jnp.sum(conv, axis=(1, 2, 3)), jnp.sum(conv * conv, axis=(1, 2,...  38.9 us
    dot_general x27, matrix products, contract(): jnp.einsum('oxyz,ixyz->oi', left, slab, precision=lax.Precision.HIGHEST)  22.7 us
    ppermute x6, waiting for transfers between devices, with_halo(): lax.ppermute(lax.slice_in_dim(block, block.shape[dim] - width, None, axis...  7.88 us
    ppermute x6, starting transfers between devices, with_halo(): lax.ppermute(lax.slice_in_dim(block, block.shape[dim] - width, None, axis...  7.03 us
    ppermute x6, starting transfers between devices, with_halo(): lax.ppermute(lax.slice_in_dim(block, 0, width, axis=dim), axis, backward)  6.81 us
  transfers between devices with their start and end apart: 12, of which 5 were waited for; matrix products, arithmetic and copies ran while one was open for 14% of the time, Pallas kernels for 0%

commit v1 on v0

--- a/solution.py
+++ b/solution.py
@@ -51,7 +51,10 @@
                     weight[:, :, first, second, third], window(padded, first, second, third)
                 )
     first_sum, square_sum = lax.psum(
-        (jnp.sum(conv, axis=(1, 2, 3)), jnp.sum(conv * conv, axis=(1, 2, 3))), ("gx", "gy", "gz")
+        lax.psum(
+            (jnp.sum(conv, axis=(1, 2, 3)), jnp.sum(conv * conv, axis=(1, 2, 3))), ("gy", "gz")
+        ),
+        "gx",
     )
     mean = first_sum / count
     var = square_sum / count - mean * mean

time: 255 us -> 250 us (0.980)
  blocking collectives: 121 us -> 117 us
    psum x1, blocking collectives: 38.9 us -> 30.9 us  [shards(): lax.psum((jnp.sum(conv, axis=(1, 2, 3)), jnp.sum(conv * conv, axis=(1, 2,...]
    psum x0 -> x1, blocking collectives: none -> 4.91 us  [shards(): lax.psum(lax.psum((jnp.sum(conv, axis=(1, 2, 3)), jnp.sum(conv * conv, ax...]
    psum x1, blocking collectives: 40.5 us -> 36.9 us  [shards(): lax.psum((jnp.sum(act_grad * normed, axis=(1, 2, 3)), jnp.sum(act_grad, a...]
    psum x1, blocking collectives: 41.9 us -> 44.8 us  [shards(): lax.psum(jnp.stack(pieces, axis=2).reshape(chans, chans, 3, 3, 3), ('gx',...]
  transfers between devices with their start and end apart: 12 -> 12, of which waited for: 5 -> 6; matrix products, arithmetic and copies ran while one was open for 14% -> 14% of each run, Pallas kernels for 0% -> 0%
where the time goes in v1:
time: 250 us; the launch traced here: 246 us
  blocking collectives  117 us (47%)
  matrix products  78.7 us (31%)
  local copies, waits for them, and re-layouts  15.7 us (6%)
  starting transfers between devices  13.7 us (5%)
  waiting for transfers between devices  10.3 us (4%)
  other arithmetic  7.77 us (3%)
    dot_general x54, matrix products, mix(): jnp.einsum('oi,ixyz->oxyz', kernel, slab, precision=lax.Precision.HIGHEST)  56 us
    psum x1, blocking collectives, shards(): lax.psum(jnp.stack(pieces, axis=2).reshape(chans, chans, 3, 3, 3), ('gx',...  44.8 us
    psum x1, blocking collectives, shards(): lax.psum((jnp.sum(act_grad * normed, axis=(1, 2, 3)), jnp.sum(act_grad, a...  36.9 us
    psum x1, blocking collectives, shards(): lax.psum((jnp.sum(conv, axis=(1, 2, 3)), jnp.sum(conv * conv, axis=(1, 2,...  30.9 us
    dot_general x27, matrix products, contract(): jnp.einsum('oxyz,ixyz->oi', left, slab, precision=lax.Precision.HIGHEST)  22.7 us
    ppermute x6, starting transfers between devices, with_halo(): lax.ppermute(lax.slice_in_dim(block, block.shape[dim] - width, None, axis...  7.46 us
    ppermute x6, waiting for transfers between devices, with_halo(): lax.ppermute(lax.slice_in_dim(block, block.shape[dim] - width, None, axis...  6.79 us
    ppermute x6, starting transfers between devices, with_halo(): lax.ppermute(lax.slice_in_dim(block, 0, width, axis=dim), axis, backward)  6.23 us
  transfers between devices with their start and end apart: 12, of which 6 were waited for; matrix products, arithmetic and copies ran while one was open for 14% of the time, Pallas kernels for 0%

profile of v1, /device:TPU:0, one launch (start us, length us, event | category | flops | bytes accessed | tf_op | source)
XLA Modules:
  0.0 245.5 jit_solution(5017022611118090781)
XLA Ops:
  0.6 1.1 fusion.319
  1.7 3.0 %collective-permute-start = (f32[16,1,16,128]{3,0,2,1:T(8,128)S(1)}, f32[16,1,16,128]{3,0,2,1:T(8,128)S(1)}, u32[]{:S(2)}, u32[]{:S(2)}) collective-permute-start(f32[16,1,16,128]{3,0,2,1:T(8,128)S(1)} %copy.207), channel_id=1, source_target_pairs={{0,16},{16,0},{1,17},{17,1},{2,18},{18,2},{3,19},{19,3},{4,20},{20... | collective-permute-start | bytes 393224 | tf_op jit(solution)/shard_map/ppermute | solution.py:13
  4.9 2.7 %fusion.206 = f32[16,4,16,128]{3,0,2,1:T(8,128)} fusion(f32[16,16,3,3,3]{1,0,4,3,2:T(8,128)} %param.6, f32[16,4,16,128]{3,2,1,0:T(8,128)} %param.5), kind=kOutput, calls=%fused_computation.290 | convolution fusion | flops 25165824 | bytes 1056768 | tf_op jit(solution)/shard_map/oi,ixyz->oxyz/dot_general | solution.py:22
  7.6 1.5 collective-permute-done
  9.5 1.6 collective-permute-done.1
  11.1 1.9 collective-permute-start.2
  13.0 2.1 collective-permute-start.3
  15.1 2.1 fusion.225
  17.2 2.1 convolution_bitcast_fusion.4
  21.0 1.9 collective-permute-start.5
  23.0 2.1 fusion.85
  25.0 2.0 fusion.86
  27.1 2.1 fusion.87
  29.1 2.1 convolution_bitcast_fusion.3
  31.2 2.1 convolution_bitcast_fusion.5
  33.3 2.1 convolution_bitcast_fusion.6
  36.1 1.6 copy.51
  37.7 1.8 maximum_maximum_fusion
  47.1 1.1 convolution_bitcast_fusion.18
  51.6 1.2 fusion.312
  52.8 30.9 %all-reduce.1 = (f32[16]{0:T(128)S(1)}, f32[16]{0:T(128)S(1)}) all-reduce(f32[16]{0:T(128)S(1)} %get-tuple-element.15, f32[16]{0:T(128)S(1)} %get-tuple-element.14), channel_id=1, replica_groups=mesh['gx'=2,'gy'=4,'gz'=4] {'gy','gz'}, use_global_device_ids=true, to_apply=%region_1.0 | all-reduce | flops 32 | bytes 256 | tf_op jit(solution)/shard_map/psum | solution.py:54
  83.7 4.9 %all-reduce.2 = (f32[16]{0:T(128)S(1)}, f32[16]{0:T(128)S(1)}) all-reduce(f32[16]{0:T(128)S(1)} %get-tuple-element.18, f32[16]{0:T(128)S(1)} %get-tuple-element.19), channel_id=1, replica_groups=mesh['gx'=2,'gy'=4,'gz'=4] {'gx'}, use_global_device_ids=true, to_apply=%region_2.0 | all-reduce | flops 32 | bytes 256 | tf_op jit(solution)/shard_map/psum | solution.py:53
  88.6 2.4 fusion.311
  91.0 36.9 %all-reduce = (f32[16]{0:T(128)S(1)}, f32[16]{0:T(128)S(1)}) all-reduce(f32[16]{0:T(128)S(1)} %get-tuple-element.13, f32[16]{0:T(128)S(1)} %get-tuple-element.12), channel_id=1, replica_groups=mesh['gx'=2,'gy'=4,'gz'=4] {'gx','gy','gz'}, use_global_device_ids=true, to_apply=%region_9.0 | all-reduce | flops 32 | bytes 256 | tf_op jit(solution)/shard_map/psum | solution.py:68
  127.9 1.4 subtract_multiply_fusion
  140.8 1.0 fusion.64
  148.4 1.0 fusion.55
  153.5 44.8 %psum.55 = f32[16,16,3,3,3]{1,0,4,3,2:T(8,128)} all-reduce(f32[16,16,3,3,3]{1,0,4,3,2:T(8,128)} %bitcast.644), channel_id=1, replica_groups=mesh['gx'=2,'gy'=4,'gz'=4] {'gx','gy','gz'}, use_global_device_ids=true, to_apply=%region_10.0 | all-reduce | flops 6912 | bytes 55296 | tf_op jit(solution)/shard_map/psum | solution.py:82
  198.3 1.5 collective-permute-start.6
  200.3 1.4 fusion.204
  201.7 2.4 collective-permute-done.6
  204.2 1.4 collective-permute-done.7
  205.6 1.6 collective-permute-start.9
  207.7 1.4 fusion.78
  210.2 2.8 %collective-permute-done.8 = f32[16,6,1,128]{3,0,2,1:T(8,128)S(1)} collective-permute-done((f32[16,6,1,128]{3,0,2,1:T(8,128)S(1)}, f32[16,6,1,128]{3,0,2,1:T(8,128)S(1)}, u32[]{:S(2)}, u32[]{:S(2)}) %collective-permute-start.8) | collective-permute-done | bytes 49184 | tf_op jit(solution)/shard_map/ppermute | solution.py:13
  213.1 1.2 fusion.315
  214.4 1.8 copy.56
  217.4 1.4 fusion.177
  218.8 1.4 fusion.175
  220.2 1.4 fusion.176
  221.7 1.4 fusion.174
  223.1 1.4 convolution_bitcast_fusion.2
  224.5 1.4 convolution_bitcast_fusion
  225.9 1.6 copy.57
  227.5 1.6 copy.61
  229.1 2.0 pad_maximum_fusion.3
  242.0 1.1 fusion.46
  243.4 1.0 fusion.48
  (159 shorter events, 51.1 us)
Async XLA Ops:
  0.6 8.5 %copy-start.2 = (f32[16,4,16,128]{3,2,1,0:T(8,128)S(1)}, f32[16,4,16,128]{3,2,1,0:T(8,128)}, u32[]{:S(2)}) copy-start(f32[16,4,16,128]{3,2,1,0:T(8,128)} %param.5) | copy-start | bytes 1572868
  1.7 7.4 %collective-permute-start = (f32[16,1,16,128]{3,0,2,1:T(8,128)S(1)}, f32[16,1,16,128]{3,0,2,1:T(8,128)S(1)}, u32[]{:S(2)}, u32[]{:S(2)}) collective-permute-start(f32[16,1,16,128]{3,0,2,1:T(8,128)S(1)} %copy.207), channel_id=1, source_target_pairs={{0,16},{16,0},{1,17},{17,1},{2,18},{18,2},{3,19},{19,3},{4,20},{20... | collective-permute-start | bytes 393224 | tf_op jit(solution)/shard_map/ppermute | solution.py:13
  4.8 6.3 %collective-permute-start.1 = (f32[16,1,16,128]{3,0,2,1:T(8,128)S(1)}, f32[16,1,16,128]{3,0,2,1:T(8,128)S(1)}, u32[]{:S(2)}, u32[]{:S(2)}) collective-permute-start(f32[16,1,16,128]{3,0,2,1:T(8,128)S(1)} %copy.208), channel_id=1, source_target_pairs={{16,0},{0,16},{17,1},{1,17},{18,2},{2,18},{19,3},{3,19},{20,4},{4,... | collective-permute-start | bytes 393224 | tf_op jit(solution)/shard_map/ppermute | solution.py:16
  9.5 9.8 %copy-start.7 = (f32[16,5,16,128]{3,0,2,1:T(8,128)}, f32[16,5,16,128]{3,0,2,1:T(8,128)S(1)}, u32[]{:S(2)}) copy-start(f32[16,5,16,128]{3,0,2,1:T(8,128)S(1)} %get-tuple-element.39) | copy-start | bytes 1966084
  11.1 8.1 %copy-start.5 = (f32[16,5,16,128]{3,0,2,1:T(8,128)}, f32[16,5,16,128]{3,0,2,1:T(8,128)S(1)}, u32[]{:S(2)}) copy-start(f32[16,5,16,128]{3,0,2,1:T(8,128)S(1)} %get-tuple-element.46) | copy-start | bytes 1966084
  11.1 8.1 %collective-permute-start.2 = (f32[16,6,1,128]{3,0,2,1:T(8,128)S(1)}, f32[16,6,1,128]{3,0,2,1:T(8,128)S(1)}, u32[]{:S(2)}, u32[]{:S(2)}) collective-permute-start(f32[16,6,1,128]{3,0,2,1:T(8,128)S(1)} %get-tuple-element.35), channel_id=1, source_target_pairs={{0,4},{4,8},{8,12},{12,0},{1,5},{5,9},{9,13},{13,1},{2,6},{6,10},{... | collective-permute-start | bytes 147464 | tf_op jit(solution)/shard_map/ppermute | solution.py:13
  13.0 6.2 %collective-permute-start.3 = (f32[16,6,1,128]{3,0,2,1:T(8,128)S(1)}, f32[16,6,1,128]{3,0,2,1:T(8,128)S(1)}, u32[]{:S(2)}, u32[]{:S(2)}) collective-permute-start(f32[16,6,1,128]{3,0,2,1:T(8,128)S(1)} %get-tuple-element.36), channel_id=1, source_target_pairs={{4,0},{8,4},{12,8},{0,12},{5,1},{9,5},{13,9},{1,13},{6,2},{10,6},{... | collective-permute-start | bytes 147464 | tf_op jit(solution)/shard_map/ppermute | solution.py:16
  20.3 15.0 %collective-permute-start.4 = (f32[16,6,18,1]{2,0,3,1:T(8,128)S(1)}, f32[16,6,18,1]{2,0,3,1:T(8,128)S(1)}, u32[]{:S(2)}, u32[]{:S(2)}) collective-permute-start(f32[16,6,18,1]{2,0,3,1:T(8,128)S(1)} %copy.48), channel_id=1, source_target_pairs={{0,1},{1,2},{2,3},{3,0},{4,5},{5,6},{6,7},{7,4},{8,9},{9,10},{10,1... | collective-permute-start | bytes 20744 | tf_op jit(solution)/shard_map/ppermute | solution.py:13
  21.0 15.0 %collective-permute-start.5 = (f32[16,6,18,1]{2,0,3,1:T(8,128)S(1)}, f32[16,6,18,1]{2,0,3,1:T(8,128)S(1)}, u32[]{:S(2)}, u32[]{:S(2)}) collective-permute-start(f32[16,6,18,1]{2,0,3,1:T(8,128)S(1)} %copy.50), channel_id=1, source_target_pairs={{1,0},{2,1},{3,2},{0,3},{5,4},{6,5},{7,6},{4,7},{9,8},{10,9},{11,1... | collective-permute-start | bytes 20744 | tf_op jit(solution)/shard_map/ppermute | solution.py:16
  37.7 1.8 copy-start.26
  39.5 11.6 %copy-start = (f32[16,6,18,129]{3,0,2,1:T(8,128)}, f32[16,6,18,129]{3,0,2,1:T(8,128)S(1)}, u32[]{:S(2)}) copy-start(f32[16,6,18,129]{3,0,2,1:T(8,128)S(1)} %get-tuple-element.30) | copy-start | bytes 2674948
  48.2 1.9 copy-start.11
  48.2 1.9 copy-start.12
  48.2 1.9 copy-start.23
  48.2 1.9 copy-start.24
  48.2 1.9 copy-start.25
  50.1 1.0 copy-start.9
  50.1 1.2 copy-start.17
  50.1 1.3 copy-start.18
  50.1 1.5 copy-start.19
  51.6 37.0 %copy-start.31 = (f32[16]{0:T(128)S(1)}, f32[16]{0:T(128)}, u32[]{:S(2)}) copy-start(f32[16]{0:T(128)} %param.7) | copy-start | bytes 196
  51.6 37.0 %copy-start.32 = (f32[16]{0:T(128)S(1)}, f32[16]{0:T(128)}, u32[]{:S(2)}) copy-start(f32[16]{0:T(128)} %param.8) | copy-start | bytes 196
  52.8 75.1 %copy-start.4 = (f32[16,4,16,128]{3,0,2,1:T(8,128)}, f32[16,4,16,128]{3,0,2,1:T(8,128)S(1)}, u32[]{:S(2)}) copy-start(f32[16,4,16,128]{3,0,2,1:T(8,128)S(1)} %get-tuple-element.49) | copy-start | bytes 1572868
  127.9 3.7 %copy-start.33 = (f32[16]{0:T(128)}, f32[16]{0:T(128)S(1)}, u32[]{:S(2)}) copy-start(f32[16]{0:T(128)S(1)} %get-tuple-element.16) | copy-start | bytes 196
  127.9 3.7 %copy-start.34 = (f32[16]{0:T(128)}, f32[16]{0:T(128)S(1)}, u32[]{:S(2)}) copy-start(f32[16]{0:T(128)S(1)} %get-tuple-element.17) | copy-start | bytes 196
  129.3 2.3 copy-start.1
  130.8 2.5 %copy-start.8 = (f32[16,5,16,128]{3,0,2,1:T(8,128)S(1)}, f32[16,5,16,128]{3,0,2,1:T(8,128)}, u32[]{:S(2)}) copy-start(f32[16,5,16,128]{3,0,2,1:T(8,128)} %copy-done.7) | copy-start | bytes 1966084
  138.3 2.5 %copy-start.3 = (f32[16,4,16,128]{3,2,1,0:T(8,128)S(1)}, f32[16,4,16,128]{3,2,1,0:T(8,128)}, u32[]{:S(2)}) copy-start(f32[16,4,16,128]{3,2,1,0:T(8,128)} %param.5) | copy-start | bytes 1572868
  145.9 2.5 %copy-start.6 = (f32[16,5,16,128]{3,0,2,1:T(8,128)S(1)}, f32[16,5,16,128]{3,0,2,1:T(8,128)}, u32[]{:S(2)}) copy-start(f32[16,5,16,128]{3,0,2,1:T(8,128)} %copy-done.5) | copy-start | bytes 1966084
  150.3 50.0 %copy-start.27 = (f32[16,16,3,3,3]{1,0,4,3,2:T(8,128)S(1)}, f32[16,16,3,3,3]{1,0,4,3,2:T(8,128)}, u32[]{:S(2)}) copy-start(f32[16,16,3,3,3]{1,0,4,3,2:T(8,128)} %param.6) | copy-start | bytes 82948
  151.1 47.2 %copy-start.30 = (f32[16,1,16,128]{3,0,2,1:T(8,128)S(1)}, f32[16,1,16,128]{3,0,2,1:T(8,128)}, u32[]{:S(2)}) copy-start(f32[16,1,16,128]{3,0,2,1:T(8,128)} %get-tuple-element.37) | copy-start | bytes 393220
  151.1 48.7 %copy-start.29 = (f32[16,1,16,128]{3,0,2,1:T(8,128)S(1)}, f32[16,1,16,128]{3,0,2,1:T(8,128)}, u32[]{:S(2)}) copy-start(f32[16,1,16,128]{3,0,2,1:T(8,128)} %get-tuple-element.38) | copy-start | bytes 393220
  152.8 0.7 copy-start.28
  198.3 5.9 %collective-permute-start.6 = (f32[16,1,16,128]{3,0,2,1:T(8,128)S(1)}, f32[16,1,16,128]{3,0,2,1:T(8,128)S(1)}, u32[]{:S(2)}, u32[]{:S(2)}) collective-permute-start(f32[16,1,16,128]{3,0,2,1:T(8,128)S(1)} %copy-done.30), channel_id=1, source_target_pairs={{0,16},{16,0},{1,17},{17,1},{2,18},{18,2},{3,19},{19,3},{4,20},{20... | collective-permute-start | bytes 393224 | tf_op jit(solution)/shard_map/ppermute | solution.py:13
  199.8 5.7 %collective-permute-start.7 = (f32[16,1,16,128]{3,0,2,1:T(8,128)S(1)}, f32[16,1,16,128]{3,0,2,1:T(8,128)S(1)}, u32[]{:S(2)}, u32[]{:S(2)}) collective-permute-start(f32[16,1,16,128]{3,0,2,1:T(8,128)S(1)} %copy-done.29), channel_id=1, source_target_pairs={{16,0},{0,16},{17,1},{1,17},{18,2},{2,18},{19,3},{3,19},{20,4},{4,... | collective-permute-start | bytes 393224 | tf_op jit(solution)/shard_map/ppermute | solution.py:16
  205.6 4.7 %collective-permute-start.9 = (f32[16,6,1,128]{3,0,2,1:T(8,128)S(1)}, f32[16,6,1,128]{3,0,2,1:T(8,128)S(1)}, u32[]{:S(2)}, u32[]{:S(2)}) collective-permute-start(f32[16,6,1,128]{3,0,2,1:T(8,128)S(1)} %get-tuple-element.34), channel_id=1, source_target_pairs={{4,0},{8,4},{12,8},{0,12},{5,1},{9,5},{13,9},{1,13},{6,2},{10,6},{... | collective-permute-start | bytes 147464 | tf_op jit(solution)/shard_map/ppermute | solution.py:16
  207.2 5.9 %collective-permute-start.8 = (f32[16,6,1,128]{3,0,2,1:T(8,128)S(1)}, f32[16,6,1,128]{3,0,2,1:T(8,128)S(1)}, u32[]{:S(2)}, u32[]{:S(2)}) collective-permute-start(f32[16,6,1,128]{3,0,2,1:T(8,128)S(1)} %get-tuple-element.33), channel_id=1, source_target_pairs={{0,4},{4,8},{8,12},{12,0},{1,5},{5,9},{9,13},{13,1},{2,6},{6,10},{... | collective-permute-start | bytes 147464 | tf_op jit(solution)/shard_map/ppermute | solution.py:13
  216.2 9.7 %collective-permute-start.10 = (f32[16,6,18,1]{2,0,3,1:T(8,128)S(1)}, f32[16,6,18,1]{2,0,3,1:T(8,128)S(1)}, u32[]{:S(2)}, u32[]{:S(2)}) collective-permute-start(f32[16,6,18,1]{2,0,3,1:T(8,128)S(1)} %copy.56), channel_id=1, source_target_pairs={{1,0},{2,1},{3,2},{0,3},{5,4},{6,5},{7,6},{4,7},{9,8},{10,9},{11,1... | collective-permute-start | bytes 20744 | tf_op jit(solution)/shard_map/ppermute | solution.py:16
  216.9 10.6 %collective-permute-start.11 = (f32[16,6,18,1]{2,0,3,1:T(8,128)S(1)}, f32[16,6,18,1]{2,0,3,1:T(8,128)S(1)}, u32[]{:S(2)}, u32[]{:S(2)}) collective-permute-start(f32[16,6,18,1]{2,0,3,1:T(8,128)S(1)} %copy.60), channel_id=1, source_target_pairs={{0,1},{1,2},{2,3},{3,0},{4,5},{5,6},{6,7},{7,4},{8,9},{9,10},{10,1... | collective-permute-start | bytes 20744 | tf_op jit(solution)/shard_map/ppermute | solution.py:13
  239.7 2.3 copy-start.10
  239.7 2.3 copy-start.13
  239.7 2.3 copy-start.20
  239.9 2.1 copy-start.21
  239.9 2.1 copy-start.22
  242.0 1.1 copy-start.14
  242.0 1.2 copy-start.15
  242.0 1.3 copy-start.16
